TPU v7x, 128 devices: a whole 4x4x4 slice. The times are simulated.
128 devices in a mesh: tx: 16 (over z, y), ty: 8 (over x, core).
Axes of the slice: x: 4, y: 4, z: 4, core: 2. Of those that a mesh axis runs over, the one named last changes fastest.
Arguments:
- fixed_volume: bfloat16 [256, 256, 128], P('tx', 'ty'), may hold values from -6 to 6
- moving_volume: bfloat16 [256, 256, 128], P('tx', 'ty'), may hold values from -6 to 6
- coarse_motion: float32 [3, 32, 32, 16], P(None, 'tx', 'ty'), may hold values from -4 to 4
- fraction_codes: int32 [3, 32, 32, 16], P(None, 'tx', 'ty'), may hold values from 0 to 7
- block_offsets: int32 [3, 32, 32, 16], P(None, 'tx', 'ty'), may hold values from -8 to 8
Outputs:
- residual: float32 [256, 256, 128], P('tx', 'ty')
- nodal: float32 [3, 32, 32, 16], P(None, 'tx', 'ty')
All inputs are finite; a program needn't handle non-finite values.
Results may differ from a plain program's by a relative error of at most 0.0003.
Values may be sent and summed in bfloat16 or wider, within the bound.
A program may use at most 64 MiB of HBM per device.

v0:
```python
import jax
import jax.numpy as jnp
from jax import lax
from jax.sharding import PartitionSpec as P

BLOCK = 8


HIGH = lax.Precision.HIGHEST


def padded(block, sides, width):
    for axis, dim in sides:
        count = lax.axis_size(axis)
        forward = [(i, i + 1) for i in range(count - 1)]
        backward = [(target, source) for source, target in forward]
        low = lax.ppermute(
            lax.slice_in_dim(block, block.shape[dim] - width, None, axis=dim), axis, forward
        )
        high = lax.ppermute(lax.slice_in_dim(block, 0, width, axis=dim), axis, backward)
        block = jnp.concatenate([low, block, high], axis=dim)
    return block


def taps(code):
    offset_value = (code.astype(jnp.float32) - (BLOCK - 1) / 2.0) / BLOCK
    return (
        jnp.maximum(-offset_value, 0.0),
        1.0 - jnp.abs(offset_value),
        jnp.maximum(offset_value, 0.0),
    )


def prolong_table(cells):
    voxel = jnp.arange(cells, dtype=jnp.int32)
    element = voxel // BLOCK
    weight_low, weight_mid, weight_high = taps(voxel % BLOCK)
    column = jnp.arange(cells // BLOCK + 2, dtype=jnp.int32)
    table = weight_low[:, None] * (column[None, :] == element[:, None]).astype(jnp.float32)
    table = table + weight_mid[:, None] * (column[None, :] == element[:, None] + 1).astype(
        jnp.float32
    )
    table = table + weight_high[:, None] * (column[None, :] == element[:, None] + 2).astype(
        jnp.float32
    )
    return table


def warp(bricks, codes):
    result = bricks
    for direction in range(3):
        weight_low, weight_mid, weight_high = taps(codes[direction])
        extent = result.shape[direction]
        before_cells = lax.slice_in_dim(result, 0, extent - 2, axis=direction)
        centre_cells = lax.slice_in_dim(result, 1, extent - 1, axis=direction)
        after_cells = lax.slice_in_dim(result, 2, extent, axis=direction)
        result = weight_low * before_cells + weight_mid * centre_cells + weight_high * after_cells
    return result


def prolong(coarse, table_x, table_y, table_z):
    spread = jnp.einsum("xi,cijk->cxjk", table_x, coarse, precision=HIGH)
    spread = jnp.einsum("yj,cxjk->cxyk", table_y, spread, precision=HIGH)
    return jnp.einsum("zk,cxyk->cxyz", table_z, spread, precision=HIGH)


def restrict(fine, table_x, table_y, table_z):
    folded = jnp.einsum("zk,cxyz->cxyk", table_z, fine, precision=HIGH)
    folded = jnp.einsum("yj,cxyk->cxjk", table_y, folded, precision=HIGH)
    return jnp.einsum("xi,cxjk->cijk", table_x, folded, precision=HIGH)


def per_device(fixed_volume, moving_volume, coarse_motion, fraction_codes, block_offsets):
    tile_x, tile_y, depth = fixed_volume.shape
    blocks_x = tile_x // BLOCK
    blocks_y = tile_y // BLOCK
    blocks_z = depth // BLOCK
    block_count = blocks_x * blocks_y * blocks_z
    brick_edge = BLOCK + 2
    margin = min(tile_x, tile_y) // 2 + 1
    wide = padded(moving_volume, (("tx", 0), ("ty", 1)), margin)
    wide = jnp.pad(wide, ((0, 0), (0, 0), (margin, margin)))
    flattened = wide.reshape(-1)
    line = depth + 2 * margin
    plane = (tile_y + 2 * margin) * line
    cube = jnp.arange(brick_edge, dtype=jnp.int32)
    offsets = (
        cube[:, None, None] * plane + cube[None, :, None] * line + cube[None, None, :]
    ).reshape(-1)
    shifts = block_offsets.reshape(3, -1)
    number = jnp.arange(block_count, dtype=jnp.int32)
    start_x = number // (blocks_y * blocks_z) * BLOCK + shifts[0] + margin - 1
    start_y = number // blocks_z % blocks_y * BLOCK + shifts[1] + margin - 1
    start_z = number % blocks_z * BLOCK + shifts[2] + margin - 1
    corner = start_x * plane + start_y * line + start_z
    own_bricks = flattened[offsets[:, None] + corner[None, :]]
    motion_framed = padded(coarse_motion, (("tx", 1), ("ty", 2)), 1)
    motion_framed = jnp.pad(motion_framed, ((0, 0), (0, 0), (0, 0), (1, 1)))
    table_x = prolong_table(tile_x)
    table_y = prolong_table(tile_y)
    table_z = prolong_table(depth)
    motion = prolong(motion_framed, table_x, table_y, table_z)
    fixed_framed = padded(fixed_volume, (("tx", 0), ("ty", 1)), 1)
    fixed_pad = jnp.pad(fixed_framed, ((0, 0), (0, 0), (1, 1))).astype(jnp.float32)
    fixed_field = fixed_pad[1:-1, 1:-1, 1:-1]
    grad_x = 0.5 * (fixed_pad[2:, 1:-1, 1:-1] - fixed_pad[:-2, 1:-1, 1:-1])
    grad_y = 0.5 * (fixed_pad[1:-1, 2:, 1:-1] - fixed_pad[1:-1, :-2, 1:-1])
    grad_z = 0.5 * (fixed_pad[1:-1, 1:-1, 2:] - fixed_pad[1:-1, 1:-1, :-2])
    cubes = own_bricks.astype(jnp.float32).reshape(brick_edge, brick_edge, brick_edge, -1)
    warped_blocks = warp(cubes, fraction_codes.reshape(3, -1)).reshape(-1)
    voxel_x = jnp.arange(tile_x, dtype=jnp.int32)[:, None, None]
    voxel_y = jnp.arange(tile_y, dtype=jnp.int32)[None, :, None]
    voxel_z = jnp.arange(depth, dtype=jnp.int32)[None, None, :]
    within = (voxel_x % BLOCK * BLOCK + voxel_y % BLOCK) * BLOCK + voxel_z % BLOCK
    owner = (voxel_x // BLOCK * blocks_y + voxel_y // BLOCK) * blocks_z + voxel_z // BLOCK
    warped = warped_blocks[within * block_count + owner]
    residual = warped + grad_x * motion[0] + grad_y * motion[1] + grad_z * motion[2] - fixed_field
    weighted = jnp.stack([grad_x * residual, grad_y * residual, grad_z * residual])
    extended = restrict(weighted, table_x, table_y, table_z)[:, :, :, 1:-1]
    bordered = padded(extended, (("tx", 1), ("ty", 2)), 1)
    inner = extended[:, 1:-1, 1:-1]
    inner = inner.at[:, 0].add(bordered[:, 0, 2:-2])
    inner = inner.at[:, -1].add(bordered[:, -1, 2:-2])
    inner = inner.at[:, :, 0].add(bordered[:, 2:-2, 0])
    inner = inner.at[:, :, -1].add(bordered[:, 2:-2, -1])
    inner = inner.at[:, 0, 0].add(bordered[:, 0, 0])
    inner = inner.at[:, 0, -1].add(bordered[:, 0, -1])
    inner = inner.at[:, -1, 0].add(bordered[:, -1, 0])
    inner = inner.at[:, -1, -1].add(bordered[:, -1, -1])
    return (residual, inner / 64.0)


def solution(mesh):
    placed = (
        P("tx", "ty", None),
        P("tx", "ty", None),
        P(None, "tx", "ty", None),
        P(None, "tx", "ty", None),
        P(None, "tx", "ty", None),
    )
    return jax.shard_map(
        per_device,
        mesh=mesh,
        in_specs=placed,
        out_specs=(P("tx", "ty", None), P(None, "tx", "ty", None)),
        check_vma=False,
    )
```

profile of v0, /device:TPU:97, one launch (start us, length us, event | category | flops | bytes accessed | tf_op | source)
XLA Modules:
  0.0 1231.1 jit_solution(8673544479655275258)
XLA Ops:
  0.7 1.0 fusion.109
  1.6 3.2 collective-permute-start
  4.8 4.2 collective-permute-start.1
  9.0 0.7 fusion.114
  9.7 1.9 collective-permute-start.8
  11.7 5.5 collective-permute-start.9
  17.1 0.7 fusion.110
  17.9 1.9 collective-permute-start.4
  20.1 0.7 fusion.113
  21.2 0.1 iota_add_fusion
  21.3 0.1 add.658
  21.4 0.7 negate_maximum_fusion.2
  22.3 0.2 compare_select_fusion.1
  22.6 0.2 fusion.16
  22.8 0.7 and_reduce_fusion
  23.7 4.8 collective-permute-start.10
  28.6 1.9 collective-permute-start.11
  31.1 5.8 collective-permute-start.5
  37.0 0.6 convolution_bitcast_fusion.1
  37.6 0.2 copy.11
  37.9 1.2 convolution_bitcast_fusion
  39.1 2.4 fusion.41
  41.6 3.9 collective-permute-start.6
  45.5 1.9 collective-permute-start.7
  47.6 3.6 collective-permute-start.2
  51.3 1.9 collective-permute-start.3
  53.2 1.1 fusion.22
  54.3 3.3 collective-permute-done.3
  57.6 0.8 fusion.5
  58.4 1.4 reshape.947
  59.8 784.7 %gather_fusion = bf16[128000]{0:T(1024)(128)(2,1)S(1)} fusion(bf16[248200]{0:T(1024)(128)(2,1)S(1)} %reshape.947, s32[128000]{0:T(1024)S(1)} %fusion.16), kind=kCustom, calls=%fused_computation | custom fusion | bytes 1024000 | tf_op jit(solution)/shard_map/gather | solution.py:96
  844.8 0.1 multiply_add_fusion
  845.1 362.7 %gather_fusion.1 = f32[65536]{0:T(1024)S(1)} fusion(f32[65536]{0:T(1024)S(1)} %bitcast.75, s32[65536]{0:T(1024)S(1)} %broadcast_clamp_fusion), kind=kCustom, calls=%fused_computation.1 | custom fusion | bytes 786432 | tf_op jit(solution)/shard_map/gather | solution.py:116
  1207.8 0.5 multiply_bitcast_fusion.2
  1208.4 0.3 multiply_bitcast_fusion.1
  1208.7 0.2 copy-done.7
  1209.1 0.8 fusion.6
  1210.0 0.6 fusion.37
  1210.7 0.2 convolution_bitcast_fusion.2
  1211.0 1.9 collective-permute-start.12
  1212.9 5.5 collective-permute-start.13
  1218.4 0.6 fusion.115
  1219.2 2.9 collective-permute-start.14
  1222.1 1.9 collective-permute-start.15
  1224.3 2.9 collective-permute-done.15
  1227.2 1.9 broadcast_select_fusion
  1229.1 1.4 scatter-add.35
  1230.5 0.6 copy.8
  (173 shorter events, 3.0 us)
Async XLA Ops:
  0.6 22.2 %copy-start.44 = (s32[4]{0:T(128)S(1)}, s32[4]{0:T(128)}, u32[]{:S(2)}) copy-start(s32[4]{0:T(128)} %constant.487.clone.1) | copy-start | bytes 52
  0.6 23.0 %copy-start.5 = (f32[3,2,4,16]{3,2,1,0:T(4,128)S(1)}, f32[3,2,4,16]{3,2,1,0:T(4,128)}, u32[]{:S(2)}) copy-start(f32[3,2,4,16]{3,2,1,0:T(4,128)} %param.23) | copy-start | bytes 4612
  1.6 45.8 %collective-permute-start = (bf16[9,32,128]{2,1,0:T(8,128)(2,1)S(1)}, bf16[9,32,128]{2,1,0:T(8,128)(2,1)S(1)}, u32[]{:S(2)}, u32[]{:S(2)}) collective-permute-start(bf16[9,32,128]{2,1,0:T(8,128)(2,1)S(1)} %get-tuple-element.114), channel_id=1, source_target_pairs={{0,8},{8,16},{16,24},{24,32},{32,40},{40,48},{48,56},{56,64},{64,7... | collective-permute-start | bytes 221192 | tf_op jit(solution)/shard_map/ppermute | solution.py:17
  4.8 42.7 %collective-permute-start.1 = (bf16[9,32,128]{2,1,0:T(8,128)(2,1)S(1)}, bf16[9,32,128]{2,1,0:T(8,128)(2,1)S(1)}, u32[]{:S(2)}, u32[]{:S(2)}) collective-permute-start(bf16[9,32,128]{2,1,0:T(8,128)(2,1)S(1)} %get-tuple-element.113), channel_id=1, source_target_pairs={{8,0},{16,8},{24,16},{32,24},{40,32},{48,40},{56,48},{64,56},{72,6... | collective-permute-start | bytes 221192 | tf_op jit(solution)/shard_map/ppermute | solution.py:20
  9.7 13.9 %collective-permute-start.8 = (f32[3,1,4,16]{3,2,1,0:T(4,128)S(1)}, f32[3,1,4,16]{3,2,1,0:T(4,128)S(1)}, u32[]{:S(2)}, u32[]{:S(2)}) collective-permute-start(f32[3,1,4,16]{3,2,1,0:T(4,128)S(1)} %get-tuple-element.136), channel_id=1, source_target_pairs={{0,8},{8,16},{16,24},{24,32},{32,40},{40,48},{48,56},{56,64},{64,7... | collective-permute-start | bytes 2312 | tf_op jit(solution)/shard_map/ppermute | solution.py:17
  11.7 12.0 collective-permute-start.9
  17.9 23.6 %collective-permute-start.4 = (bf16[1,32,128]{2,1,0:T(8,128)(2,1)S(1)}, bf16[1,32,128]{2,1,0:T(8,128)(2,1)S(1)}, u32[]{:S(2)}, u32[]{:S(2)}) collective-permute-start(bf16[1,32,128]{2,1,0:T(8,128)(2,1)S(1)} %get-tuple-element.116), channel_id=1, source_target_pairs={{0,8},{8,16},{16,24},{24,32},{32,40},{40,48},{48,56},{56,64},{64,7... | collective-permute-start | bytes 24584 | tf_op jit(solution)/shard_map/ppermute | solution.py:17
  19.8 18.0 %copy-start.8 = (s32[32]{0:T(128)}, s32[32]{0:T(128)S(1)}, u32[]{:S(2)}) copy-start(s32[32]{0:T(128)S(1)} %get-tuple-element.141) | copy-start | bytes 388
  19.8 19.3 %copy-start.6 = (s32[128]{0:T(128)}, s32[128]{0:T(128)S(1)}, u32[]{:S(2)}) copy-start(s32[128]{0:T(128)S(1)} %get-tuple-element.139) | copy-start | bytes 1540
  19.8 19.3 %copy-start.24 = (s32[128]{0:T(128)}, s32[128]{0:T(128)S(1)}, u32[]{:S(2)}) copy-start(s32[128]{0:T(128)S(1)} %get-tuple-element.140) | copy-start | bytes 1540
  19.9 17.0 %copy-start.12 = (s32[16]{0:T(128)}, s32[16]{0:T(128)S(1)}, u32[]{:S(2)}) copy-start(s32[16]{0:T(128)S(1)} %get-tuple-element.143) | copy-start | bytes 196
  19.9 17.0 %copy-start.14 = (s32[16]{0:T(128)}, s32[16]{0:T(128)S(1)}, u32[]{:S(2)}) copy-start(s32[16]{0:T(128)S(1)} %get-tuple-element.144) | copy-start | bytes 196
  19.9 17.0 %copy-start.16 = (f32[16]{0:T(128)}, f32[16]{0:T(128)S(1)}, u32[]{:S(2)}) copy-start(f32[16]{0:T(128)S(1)} %get-tuple-element.149) | copy-start | bytes 196
  19.9 17.0 %copy-start.18 = (f32[16]{0:T(128)}, f32[16]{0:T(128)S(1)}, u32[]{:S(2)}) copy-start(f32[16]{0:T(128)S(1)} %get-tuple-element.150) | copy-start | bytes 196
  19.9 17.0 %copy-start.20 = (s32[16]{0:T(128)}, s32[16]{0:T(128)S(1)}, u32[]{:S(2)}) copy-start(s32[16]{0:T(128)S(1)} %broadcast_add_fusion.5) | copy-start | bytes 196
  20.0 17.0 %copy-start.22 = (f32[16]{0:T(128)}, f32[16]{0:T(128)S(1)}, u32[]{:S(2)}) copy-start(f32[16]{0:T(128)S(1)} %broadcast_maximum_fusion.4) | copy-start | bytes 196
  20.0 17.8 %copy-start.26 = (f32[32]{0:T(128)}, f32[32]{0:T(128)S(1)}, u32[]{:S(2)}) copy-start(f32[32]{0:T(128)S(1)} %get-tuple-element.147) | copy-start | bytes 388
  20.0 17.8 %copy-start.28 = (f32[32]{0:T(128)}, f32[32]{0:T(128)S(1)}, u32[]{:S(2)}) copy-start(f32[32]{0:T(128)S(1)} %get-tuple-element.148) | copy-start | bytes 388
  20.0 17.8 %copy-start.30 = (s32[32]{0:T(128)}, s32[32]{0:T(128)S(1)}, u32[]{:S(2)}) copy-start(s32[32]{0:T(128)S(1)} %get-tuple-element.151) | copy-start | bytes 388
  20.0 17.8 %copy-start.32 = (s32[32]{0:T(128)}, s32[32]{0:T(128)S(1)}, u32[]{:S(2)}) copy-start(s32[32]{0:T(128)S(1)} %get-tuple-element.152) | copy-start | bytes 388
  20.0 17.8 %copy-start.34 = (f32[32]{0:T(128)}, f32[32]{0:T(128)S(1)}, u32[]{:S(2)}) copy-start(f32[32]{0:T(128)S(1)} %broadcast_maximum_fusion.3) | copy-start | bytes 388
  20.1 19.0 %copy-start.36 = (f32[128]{0:T(128)}, f32[128]{0:T(128)S(1)}, u32[]{:S(2)}) copy-start(f32[128]{0:T(128)S(1)} %get-tuple-element.145) | copy-start | bytes 1540
  20.1 19.0 %copy-start.38 = (f32[128]{0:T(128)}, f32[128]{0:T(128)S(1)}, u32[]{:S(2)}) copy-start(f32[128]{0:T(128)S(1)} %get-tuple-element.146) | copy-start | bytes 1540
  20.1 19.0 %copy-start.40 = (s32[128]{0:T(128)}, s32[128]{0:T(128)S(1)}, u32[]{:S(2)}) copy-start(s32[128]{0:T(128)S(1)} %broadcast_add_fusion.6) | copy-start | bytes 1540
  20.1 16.7 %copy-start.10 = (s32[2]{0:T(128)}, s32[2]{0:T(128)S(1)}, u32[]{:S(2)}) copy-start(s32[2]{0:T(128)S(1)} %iota_multiply_fusion) | copy-start | bytes 28
  23.5 18.0 %copy-start.42 = (f32[128]{0:T(128)}, f32[128]{0:T(128)S(1)}, u32[]{:S(2)}) copy-start(f32[128]{0:T(128)S(1)} %broadcast_maximum_fusion.5) | copy-start | bytes 1540
  23.7 7.3 collective-permute-start.10
  28.6 8.2 collective-permute-start.11
  31.1 10.5 collective-permute-start.5
  37.9 3.6 copy-start.4
  39.1 8.4 copy-start.3
  41.6 11.6 collective-permute-start.6
  45.5 7.7 collective-permute-start.7
  47.6 6.7 collective-permute-start.2
  51.3 6.4 collective-permute-start.3
  845.1 362.7 %copy-start = (f32[18,34,130]{2,1,0:T(8,128)S(1)}, f32[18,34,130]{2,1,0:T(8,128)}, u32[]{:S(2)}) copy-start(f32[18,34,130]{2,1,0:T(8,128)} %fusion.22) | copy-start | bytes 954724
  845.1 362.7 %copy-start.1 = (f32[3,16,32,128]{3,2,1,0:T(8,128)S(1)}, f32[3,16,32,128]{3,2,1,0:T(8,128)}, u32[]{:S(2)}) copy-start(f32[3,16,32,128]{3,2,1,0:T(8,128)} %fusion.41) | copy-start | bytes 2359300
  1208.3 1.6 copy-start.2
  1209.1 1.5 copy-start.15
  1209.1 1.5 copy-start.17
  1209.1 1.5 copy-start.19
  1209.1 1.5 copy-start.21
  1209.1 1.5 copy-start.23
  1210.0 8.4 copy-start.11
  1211.0 8.2 collective-permute-start.12
  1212.9 6.3 collective-permute-start.13
  1219.2 5.1 collective-permute-start.14
  1222.1 5.0 collective-permute-start.15
  (13 other events, 13.1 us)
where the time goes:
time: 1230 us
  local copies, waits for them, and re-layouts  1160 us (94%)
  starting transfers between devices  52.8 us (4%)
    gather x1, local copies, waits for them, and re-layouts, per_device(): own_bricks = flattened[offsets[:, None] + corner[None, :]]  785 us
    gather x1, local copies, waits for them, and re-layouts, per_device(): warped = warped_blocks[within * block_count + owner]  363 us
    ppermute x8, starting transfers between devices, padded(): lax.ppermute(lax.slice_in_dim(block, 0, width, axis=dim), axis, backward)  28.6 us
  transfers between devices with their start and end apart: 16, of which 2 were waited for; matrix products, arithmetic and copies ran while one was open for 1% of the time, Pallas kernels for 0%

commit v1 on v0

v1 whole, which is shorter than its diff:
```python
import functools

import jax
import jax.numpy as jnp
import numpy as np
from jax import lax
from jax.experimental import pallas as pl
from jax.experimental.pallas import tpu as pltpu
from jax.sharding import PartitionSpec as P

MESH = pl.DeviceIdType.MESH
F32 = jnp.float32
BF16 = jnp.bfloat16

DIRS = ((1, 0), (-1, 0), (1, 1), (1, -1), (-1, 1), (-1, -1), (0, 1), (0, -1))
SLOT = {d: k for k, d in enumerate(DIRS)}
FIX_DIRS = ((1, 0), (-1, 0), (0, 1), (0, -1))

EDGE = 9
PLANES = 16 + 2 * EDGE
WIN = 26
ROWS = 40


def hat(values):
    return np.maximum(0.0, 1.0 - np.abs(values))


def ghost_rows():
    return np.array([0, 1, 2, 3, -1, 4, 90, 90])


def constants():
    lane = np.arange(128)
    spread = (np.arange(128)[:, None] == lane[None, :] // 8).astype(np.float32)
    z = np.arange(128)
    along_z = hat((z[:, None] - 3.5) / 8 - np.arange(16)[None, :])
    to_nodes = np.zeros((3, 128, 128), np.float32)
    for c in range(3):
        to_nodes[c, :, 16 * c : 16 * c + 16] = along_z
    from_nodes = np.concatenate([to_nodes[c].T for c in range(3)], axis=1)
    to_nodes = to_nodes.reshape(384, 128)
    x, y = np.arange(16), np.arange(32)
    along_x = hat((x[:, None] - 3.5) / 8 - (np.arange(4)[None, :] - 1))
    along_y = hat((y[:, None] - 3.5) / 8 - ghost_rows()[None, :])
    table = (along_x[:, None, :, None] * along_y[None, :, None, :]).reshape(512, 32)
    table = np.concatenate([table, table, table, np.zeros_like(table)], axis=1)
    fold_y = np.zeros((4, 8, 4, 32), np.float32)
    for i in range(4):
        fold_y[i, :, i, :] = along_y.T
    fold_y = fold_y.reshape(32, 128)
    return [jnp.asarray(a, BF16) for a in (spread, from_nodes, table, fold_y, to_nodes)]


def split(value, parts):
    out = []
    for _ in range(parts - 1):
        piece = value.astype(BF16)
        out.append(piece)
        value = value - piece.astype(F32)
    out.append(value.astype(BF16))
    return out


def dot(a, b):
    return jnp.dot(a, b, preferred_element_type=F32)


def body(
    fixed, moving, coarse, codes, offsets, spread, from_nodes, table, fold_y, to_nodes,
    residual, nodal,
    wide, fixed_wide, fixed_f32, coarse_own, coarse_pack, coarse_in, code_v, offset_v,
    row_v, row_s, quant, quant_wide, spread_v, from_v, table_v, fold_v, to_v,
    hats, windows, known, grads, folded, node_own, node_in,
    local_sem, move_send, move_recv, fix_send, fix_recv, coarse_send, coarse_recv,
    node_send, node_recv,
):
    tx, ty = lax.axis_index("tx"), lax.axis_index("ty")
    count_x, count_y = lax.axis_size("tx"), lax.axis_size("ty")

    def has(dx, dy):
        found = None
        for step, at, count in ((dx, tx, count_x), (dy, ty, count_y)):
            if step:
                test = at > 0 if step < 0 else at < count - 1
                found = test if found is None else jnp.logical_and(found, test)
        return found

    def device(dx, dy):
        return (tx + dx, ty + dy)

    barrier = pltpu.get_barrier_semaphore()
    for d in DIRS:
        @pl.when(has(*d))
        def _(d=d):
            pl.semaphore_signal(barrier, inc=1, device_id=device(*d), device_id_type=MESH)

    local = []
    for k, (src, dst) in enumerate((
        (coarse, coarse_own), (offsets, offset_v), (codes, code_v),
        (moving, wide.at[EDGE : EDGE + 16, 16:48, :]),
        (fixed, fixed_wide.at[1:17, 8:40, :]),
        (spread, spread_v), (from_nodes, from_v), (table, table_v), (fold_y, fold_v), (to_nodes, to_v),
    )):
        copy = pltpu.make_async_copy(src, dst, local_sem.at[k])
        copy.start()
        local.append(copy)

    def span_x(dx, width, base, extent):
        if dx == 1:
            return slice(16 - width, 16), slice(base - width, base)
        if dx == -1:
            return slice(0, width), slice(base + extent, base + extent + width)
        return slice(0, extent), slice(base, base + extent)

    def span_y(dy, width, base):
        if dy == 1:
            return slice(32 - width, 32), slice(base - width, base)
        if dy == -1:
            return slice(0, width), slice(base + 32, base + 32 + width)
        return slice(0, 32), slice(base, base + 32)

    move_copy, move_zone = {}, {}
    for d in DIRS:
        sx, tx_zone = span_x(d[0], EDGE, EDGE, 16)
        sy, ty_zone = span_y(d[1], 16, 16)
        move_zone[d] = (tx_zone, ty_zone)
        k = SLOT[d]
        move_copy[d] = pltpu.make_async_remote_copy(
            src_ref=moving.at[sx, sy, :], dst_ref=wide.at[tx_zone, ty_zone, :],
            send_sem=move_send.at[k], recv_sem=move_recv.at[k],
            device_id=device(*d), device_id_type=MESH,
        )
    fix_copy, fix_zone = {}, {}
    for k, d in enumerate(FIX_DIRS):
        sx, tx_zone = span_x(d[0], 1, 1, 16)
        sy, ty_zone = span_y(d[1], 8, 8)
        fix_zone[d] = (tx_zone, ty_zone)
        fix_copy[d] = pltpu.make_async_remote_copy(
            src_ref=fixed.at[sx, sy, :], dst_ref=fixed_wide.at[tx_zone, ty_zone, :],
            send_sem=fix_send.at[k], recv_sem=fix_recv.at[k],
            device_id=device(*d), device_id_type=MESH,
        )

    def slab(dx):
        return {1: slice(1, 2), -1: slice(0, 1), 0: slice(0, 2)}[dx]

    coarse_copy = {}
    for d in DIRS:
        k = SLOT[d]
        part = slab(d[0])
        coarse_copy[d] = pltpu.make_async_remote_copy(
            src_ref=coarse_pack.at[part], dst_ref=coarse_in.at[k, 0 : part.stop - part.start],
            send_sem=coarse_send.at[k], recv_sem=coarse_recv.at[k],
            device_id=device(*d), device_id_type=MESH,
        )

    local[0].wait()
    coarse_pack[...] = jnp.zeros_like(coarse_pack)
    for c in range(3):
        for X in range(2):
            coarse_pack[X, 0:4, 16 * c : 16 * c + 16] = coarse_own[c, X]

    expected = 0
    for d in DIRS:
        expected = expected + jnp.where(has(*d), 1, 0)
    pl.semaphore_wait(barrier, expected)

    def start(copies, d):
        @pl.when(has(*d))
        def _():
            copies[d].start()

    def arrive(copies, d):
        @pl.when(has(-d[0], -d[1]))
        def _():
            copies[d].wait_recv()

    def absent(d):
        return jnp.logical_not(has(-d[0], -d[1]))

    for d in DIRS[:2]:
        start(coarse_copy, d)
        start(fix_copy, d)
        start(move_copy, d)
    for d in DIRS[2:6]:
        start(coarse_copy, d)
        start(move_copy, d)
    for d in DIRS[6:]:
        start(coarse_copy, d)
        start(fix_copy, d)
        start(move_copy, d)

    for d in DIRS:
        @pl.when(absent(d))
        def _(d=d):
            zx, zy = move_zone[d]
            wide[zx, zy, :] = jnp.zeros((zx.stop - zx.start, zy.stop - zy.start, 128), BF16)
            coarse_in[SLOT[d]] = jnp.zeros((2, 8, 128), F32)
            node_in[SLOT[d]] = jnp.zeros((2, 8, 128), F32)
            if d in fix_zone:
                fx, fy = fix_zone[d]
                fixed_wide[fx, fy, :] = jnp.zeros((fx.stop - fx.start, fy.stop - fy.start, 128), BF16)

    local[1].wait()
    local[2].wait()
    quant[...] = jnp.zeros_like(quant)
    row_v[...] = jnp.zeros_like(row_v)
    for X in range(2):
        late = [jnp.where(code_v[c, X] >= 4, 1, 0) for c in range(3)]
        base_x = offset_v[0, X] + late[0] - 1
        base_y = offset_v[1, X] + late[1] - 1
        column = lax.broadcasted_iota(jnp.int32, (4, 16), 0) + 4 * X
        row_v[4 * X : 4 * X + 4, 0:16] = (
            column * (WIN * ROWS) + (base_x + EDGE) * ROWS + base_y + 16
        )
        step = [(code_v[c, X].astype(F32) - 3.5) * 0.125 for c in range(3)]
        quant[4 * X : 4 * X + 4, 0:16] = offset_v[2, X].astype(F32) + step[2]
        for q in range(2):
            quant[8 + 8 * q + 4 * X : 12 + 8 * q + 4 * X, 0:16] = (
                step[q] + 1.0 - late[q].astype(F32)
            )
    to_scalar = pltpu.make_async_copy(row_v, row_s, local_sem.at[10])
    to_scalar.start()

    local[5].wait()
    quant_wide[...] = dot(quant[...].astype(BF16), spread_v[...])

    lane = lax.broadcasted_iota(jnp.int32, (128, 128), 1).astype(F32)
    depth = lax.broadcasted_iota(jnp.int32, (128, 128), 0).astype(F32)
    gap = depth - lane
    for pair in range(4):
        for side in range(2):
            col = 2 * pair + side
            weights = jnp.maximum(0.0, 1.0 - jnp.abs(gap - quant_wide[col : col + 1, :]))
            hats[pair, :, 128 * side : 128 * side + 128] = weights.astype(BF16)

    def interpolate_z(first, last, group):
        for X in range(2):
            low, high = max(first, 8 * X), min(last, 8 * X + WIN)
            if low >= high:
                continue
            planes = high - low
            rows = wide[low:high, 16 * group : 16 * group + 16, :].reshape(planes * 16, 128)
            for p in range(2):
                at = group - p
                if at < 0 or at > 2:
                    continue
                pair = 2 * X + p
                result = dot(rows, hats[pair]).reshape(planes, 16, 256)
                for side in range(2):
                    begin = 16 * at - 8 * side
                    cut = max(0, -begin)
                    stop = min(16, ROWS - begin)
                    for n in range(planes):
                        to = (2 * pair + side) * WIN * ROWS + (low + n - 8 * X) * ROWS + begin
                        windows[to + cut : to + stop, :] = result[
                            n, cut:stop, 128 * side : 128 * side + 128
                        ]

    local[3].wait()
    own_x = (EDGE, EDGE + 16)
    interpolate_z(*own_x, 1)
    interpolate_z(*own_x, 2)

    for d in DIRS:
        arrive(coarse_copy, d)
    row = lax.broadcasted_iota(jnp.int32, (8, 128), 0)

    def framed(centre, low, high):
        ghost = jnp.where(row == 4, pltpu.roll(low, 1, 0), jnp.where(row == 5, pltpu.roll(high, 5, 0), 0.0))
        return jnp.where(row < 4, centre, ghost)

    nodes = [
        framed(coarse_in[SLOT[1, 0], 0], coarse_in[SLOT[1, 1], 0], coarse_in[SLOT[1, -1], 0]),
        framed(coarse_pack[0], coarse_in[SLOT[0, 1], 0], coarse_in[SLOT[0, -1], 0]),
        framed(coarse_pack[1], coarse_in[SLOT[0, 1], 1], coarse_in[SLOT[0, -1], 1]),
        framed(coarse_in[SLOT[-1, 0], 0], coarse_in[SLOT[-1, 1], 0], coarse_in[SLOT[-1, -1], 0]),
    ]
    local[6].wait()
    nodes = jnp.concatenate(split(jnp.concatenate(nodes, axis=0), 3), axis=0)
    spread_z = dot(nodes, from_v[...])
    spread_z = spread_z[0:32] + spread_z[32:64] + spread_z[64:96]
    pieces = split(spread_z, 3)
    stacked = jnp.concatenate(pieces + [jnp.zeros_like(pieces[0])], axis=0)

    for d in FIX_DIRS:
        arrive(fix_copy, d)
    local[4].wait()
    fixed_f32[...] = fixed_wide[...].astype(F32)
    local[7].wait()
    last_lane = lax.broadcasted_iota(jnp.int32, (32, 128), 1)
    for chunk in range(4):
        motion = dot(table_v[128 * chunk : 128 * chunk + 128, :], stacked)
        for n in range(4):
            at = 4 * chunk + n
            centre = fixed_f32[at + 1, 8:40, :]
            grad_x = 0.5 * (fixed_f32[at + 2, 8:40, :] - fixed_f32[at, 8:40, :])
            grad_y = 0.5 * (fixed_f32[at + 1, 9:41, :] - fixed_f32[at + 1, 7:39, :])
            after = jnp.where(last_lane == 127, 0.0, pltpu.roll(centre, 127, 1))
            before = jnp.where(last_lane == 0, 0.0, pltpu.roll(centre, 1, 1))
            grad_z = 0.5 * (after - before)
            total = -centre
            for c, grad in enumerate((grad_x, grad_y, grad_z)):
                grads[c, at] = grad
                total = total + grad * motion[32 * n : 32 * n + 32, 128 * c : 128 * c + 128]
            known[at] = total

    arrive(move_copy, (0, 1))
    interpolate_z(*own_x, 0)
    arrive(move_copy, (0, -1))
    interpolate_z(*own_x, 3)
    below, above = (0, EDGE), (EDGE + 16, PLANES)
    arrive(move_copy, (1, 0))
    interpolate_z(*below, 1)
    interpolate_z(*below, 2)
    arrive(move_copy, (-1, 0))
    interpolate_z(*above, 1)
    interpolate_z(*above, 2)
    arrive(move_copy, (1, 1))
    interpolate_z(*below, 0)
    arrive(move_copy, (1, -1))
    interpolate_z(*below, 3)
    arrive(move_copy, (-1, 1))
    interpolate_z(*above, 0)
    arrive(move_copy, (-1, -1))
    interpolate_z(*above, 3)
    to_scalar.wait()

    block_of_lane = lax.broadcasted_iota(jnp.int32, (8, 128), 1) // 8
    inner = [1.0 - abs(l - 3.5) / 8 for l in range(8)]
    outer = [abs(l - 3.5) / 8 for l in range(8)]

    def per_row(Y, carry):
        sums = [[None] * 4 for _ in range(3)]
        y8 = pl.multiple_of(8 * Y, 8)

        def add(c, i, value):
            sums[c][i] = value if sums[c][i] is None else sums[c][i] + value

        for X in range(2):
            col = 4 * X + Y
            first, second = [None] * 9, [None] * 9
            for Z in range(16):
                begin = row_s[col, Z]
                mine = block_of_lane == Z
                for n in range(9):
                    a = windows[pl.ds(begin + ROWS * n, 8), :]
                    b = windows[pl.ds(begin + ROWS * n + 1, 8), :]
                    first[n] = a if Z == 0 else jnp.where(mine, a, first[n])
                    second[n] = b if Z == 0 else jnp.where(mine, b, second[n])
            weight_x = jnp.broadcast_to(quant_wide[pl.ds(8 + col, 1), :], (8, 128))
            weight_y = jnp.broadcast_to(quant_wide[pl.ds(16 + col, 1), :], (8, 128))
            lines = [first[n] + weight_y * (second[n] - first[n]) for n in range(9)]
            for l in range(8):
                warped = lines[l] + weight_x * (lines[l + 1] - lines[l])
                at = 8 * X + l
                value = warped + known[at, pl.ds(y8, 8), :]
                residual[at, pl.ds(y8, 8), :] = value
                for c in range(3):
                    term = grads[c, at, pl.ds(y8, 8), :] * value
                    add(c, X + 1, term * inner[l])
                    add(c, X if l < 4 else X + 2, term * outer[l])
        for c in range(3):
            for i in range(4):
                folded[pl.ds(pl.multiple_of(32 * i + y8, 8), 8), 128 * c : 128 * c + 128] = sums[c][i]
        return carry

    lax.fori_loop(0, 4, per_row, 0)

    local[8].wait()
    local[9].wait()
    high, low = split(folded[...], 2)
    rows = dot(fold_v[...], high) + dot(fold_v[...], low)
    high, low = split(rows, 2)
    ends = (dot(high, to_v[...]) + dot(low, to_v[...])) * (1.0 / 64.0)
    node_own[...] = ends.reshape(4, 8, 128)

    node_copy = {}
    for d in DIRS:
        k = SLOT[d]
        part = {1: slice(3, 4), -1: slice(0, 1), 0: slice(1, 3)}[d[0]]
        node_copy[d] = pltpu.make_async_remote_copy(
            src_ref=node_own.at[part], dst_ref=node_in.at[k, 0 : part.stop - part.start],
            send_sem=node_send.at[k], recv_sem=node_recv.at[k],
            device_id=device(*d), device_id_type=MESH,
        )
        start(node_copy, d)
    for d in DIRS:
        arrive(node_copy, d)

    def summed(dy):
        own = [node_own[1], node_own[2]] if dy == 0 else [node_in[SLOT[0, dy], X] for X in range(2)]
        return [own[0] + node_in[SLOT[1, dy], 0], own[1] + node_in[SLOT[-1, dy], 0]]

    centre, from_low, from_high = summed(0), summed(1), summed(-1)
    for X in range(2):
        value = centre[X]
        value = value + jnp.where(row == 0, pltpu.roll(from_low[X], 3, 0), 0.0)
        value = value + jnp.where(row == 3, pltpu.roll(from_high[X], 7, 0), 0.0)
        for c in range(3):
            nodal[c, X] = value[0:4, 16 * c : 16 * c + 16]

    for copies, dirs in ((coarse_copy, DIRS), (fix_copy, FIX_DIRS), (move_copy, DIRS), (node_copy, DIRS)):
        for d in dirs:
            @pl.when(has(*d))
            def _(copies=copies, d=d):
                copies[d].wait_send()


def per_device(fixed_volume, moving_volume, coarse_motion, fraction_codes, block_offsets):
    hbm = pl.BlockSpec(memory_space=pltpu.HBM)
    vmem = pl.BlockSpec(memory_space=pltpu.VMEM)
    dma = pltpu.SemaphoreType.DMA
    return pl.pallas_call(
        body,
        out_shape=(
            jax.ShapeDtypeStruct((16, 32, 128), F32),
            jax.ShapeDtypeStruct((3, 2, 4, 16), F32),
        ),
        in_specs=[hbm] * 10,
        out_specs=(vmem, vmem),
        scratch_shapes=[
            pltpu.VMEM((PLANES, 64, 128), BF16),
            pltpu.VMEM((18, 48, 128), BF16),
            pltpu.VMEM((18, 48, 128), F32),
            pltpu.VMEM((3, 2, 4, 16), F32),
            pltpu.VMEM((2, 8, 128), F32),
            pltpu.VMEM((8, 2, 8, 128), F32),
            pltpu.VMEM((3, 2, 4, 16), jnp.int32),
            pltpu.VMEM((3, 2, 4, 16), jnp.int32),
            pltpu.VMEM((8, 128), jnp.int32),
            pltpu.SMEM((8, 128), jnp.int32),
            pltpu.VMEM((32, 128), F32),
            pltpu.VMEM((32, 128), F32),
            pltpu.VMEM((128, 128), BF16),
            pltpu.VMEM((128, 384), BF16),
            pltpu.VMEM((512, 128), BF16),
            pltpu.VMEM((32, 128), BF16),
            pltpu.VMEM((384, 128), BF16),
            pltpu.VMEM((4, 128, 256), BF16),
            pltpu.VMEM((8 * WIN * ROWS, 128), F32),
            pltpu.VMEM((16, 32, 128), F32),
            pltpu.VMEM((3, 16, 32, 128), F32),
            pltpu.VMEM((128, 384), F32),
            pltpu.VMEM((4, 8, 128), F32),
            pltpu.VMEM((8, 2, 8, 128), F32),
            dma((11,)), dma((8,)), dma((8,)), dma((4,)), dma((4,)), dma((8,)), dma((8,)),
            dma((8,)), dma((8,)),
        ],
        compiler_params=pltpu.CompilerParams(
            collective_id=0, has_side_effects=True, vmem_limit_bytes=32 << 20
        ),
    )(fixed_volume, moving_volume, coarse_motion, fraction_codes, block_offsets, *constants())


def solution(mesh):
    placed = (
        P("tx", "ty", None),
        P("tx", "ty", None),
        P(None, "tx", "ty", None),
        P(None, "tx", "ty", None),
        P(None, "tx", "ty", None),
    )
    return jax.shard_map(
        per_device,
        mesh=mesh,
        in_specs=placed,
        out_specs=(P("tx", "ty", None), P(None, "tx", "ty", None)),
        check_vma=False,
    )
```

time: 1230 us -> 28.7 us (0.02)
  local copies, waits for them, and re-layouts: 1160 us -> 9.37 us
  starting transfers between devices: 52.8 us -> 0 us
  Pallas kernels: 0 us -> 18.1 us
    gather x2 -> x0, local copies, waits for them, and re-layouts: 1150 us -> none  [the longest x1 785 us: per_device(): own_bricks = flattened[offsets[:, None] + corner[None, :]]]
    ppermute x16 -> x0, starting transfers between devices: 52.8 us -> none  [the longest x8 28.6 us: padded(): lax.ppermute(lax.slice_in_dim(block, 0, width, axis=dim), axis, backward)]
    pallas_call x0 -> x1, Pallas kernels: none -> 18.1 us  [per_device(): pl.pallas_call(body, out_shape=(jax.ShapeDtypeStruct((16, 32, 128), F32),...]
  transfers between devices with their start and end apart: 16 -> 0, of which waited for: 2 -> 0; matrix products, arithmetic and copies ran while one was open for 1% -> 0% of each run, Pallas kernels for 0% -> 0%
where the time goes in v1:
time: 28.7 us; the launch traced here: 28.2 us
  Pallas kernels  18.1 us (63%)
  local copies, waits for them, and re-layouts  9.37 us (33%)
  between operations  0.66 us (2%)
    pallas_call x1, Pallas kernels, per_device(): pl.pallas_call(body, out_shape=(jax.ShapeDtypeStruct((16, 32, 128), F32),...  18.1 us
    unnamed x22, local copies, waits for them, and re-layouts  9.37 us

profile of v1, /device:TPU:97, one launch (start us, length us, event | category | flops | bytes accessed | tf_op | source)
XLA Modules:
  0.0 28.2 jit_solution(1040276627942910313)
XLA Ops:
  0.6 0.0 copy-start
  0.6 0.9 %copy-done = bf16[16,32,128]{2,1,0:T(8,128)(2,1)S(1)} copy-done((bf16[16,32,128]{2,1,0:T(8,128)(2,1)S(1)}, bf16[16,32,128]{2,1,0:T(8,128)(2,1)}, u32[]{:S(2)}) %copy-start) | copy-done | bytes 131096
  1.5 0.0 copy-start.1
  1.5 0.9 %copy-done.1 = bf16[16,32,128]{2,1,0:T(8,128)(2,1)S(1)} copy-done((bf16[16,32,128]{2,1,0:T(8,128)(2,1)S(1)}, bf16[16,32,128]{2,1,0:T(8,128)(2,1)}, u32[]{:S(2)}) %copy-start.1) | copy-done | bytes 131096
  2.4 0.0 copy-start.2
  2.4 0.9 %copy-done.2 = bf16[512,128]{1,0:T(8,128)(2,1)S(1)} copy-done((bf16[512,128]{1,0:T(8,128)(2,1)S(1)}, bf16[512,128]{1,0:T(8,128)(2,1)}, u32[]{:S(2)}) %copy-start.2) | copy-done | bytes 131096
  3.3 0.0 copy-start.3
  3.3 0.9 %copy-done.3 = bf16[384,128]{1,0:T(8,128)(2,1)S(1)} copy-done((bf16[384,128]{1,0:T(8,128)(2,1)S(1)}, bf16[384,128]{1,0:T(8,128)(2,1)}, u32[]{:S(2)}) %copy-start.3) | copy-done | bytes 98328
  4.2 0.0 copy-start.4
  4.2 0.9 %copy-done.4 = bf16[128,384]{1,0:T(8,128)(2,1)S(1)} copy-done((bf16[128,384]{1,0:T(8,128)(2,1)S(1)}, bf16[128,384]{1,0:T(8,128)(2,1)}, u32[]{:S(2)}) %copy-start.4) | copy-done | bytes 98328
  5.1 0.0 copy-start.5
  5.1 0.8 %copy-done.5 = bf16[128,128]{1,0:T(8,128)(2,1)S(1)} copy-done((bf16[128,128]{1,0:T(8,128)(2,1)S(1)}, bf16[128,128]{1,0:T(8,128)(2,1)}, u32[]{:S(2)}) %copy-start.5) | copy-done | bytes 32792
  5.9 0.0 copy-start.6
  5.9 0.7 %copy-done.6 = f32[3,2,4,16]{3,2,1,0:T(4,128)S(1)} copy-done((f32[3,2,4,16]{3,2,1,0:T(4,128)S(1)}, f32[3,2,4,16]{3,2,1,0:T(4,128)}, u32[]{:S(2)}) %copy-start.6) | copy-done | bytes 1560
  6.6 0.0 copy-start.7
  6.6 0.7 %copy-done.7 = s32[3,2,4,16]{3,2,1,0:T(4,128)S(1)} copy-done((s32[3,2,4,16]{3,2,1,0:T(4,128)S(1)}, s32[3,2,4,16]{3,2,1,0:T(4,128)}, u32[]{:S(2)}) %copy-start.7) | copy-done | bytes 1560
  7.3 0.0 copy-start.8
  7.3 0.7 %copy-done.8 = s32[3,2,4,16]{3,2,1,0:T(4,128)S(1)} copy-done((s32[3,2,4,16]{3,2,1,0:T(4,128)S(1)}, s32[3,2,4,16]{3,2,1,0:T(4,128)}, u32[]{:S(2)}) %copy-start.8) | copy-done | bytes 1560
  8.0 0.0 copy-start.9
  8.0 0.7 %copy-done.9 = bf16[32,128]{1,0:T(8,128)(2,1)S(1)} copy-done((bf16[32,128]{1,0:T(8,128)(2,1)S(1)}, bf16[32,128]{1,0:T(8,128)(2,1)}, u32[]{:S(2)}) %copy-start.9) | copy-done | bytes 8216
  8.7 18.1 %shard_map.113 = (f32[16,32,128]{2,1,0:T(8,128)S(1)}, f32[3,2,4,16]{3,2,1,0:T(4,128)S(1)}) custom-call(bf16[16,32,128]{2,1,0:T(8,128)(2,1)S(1)} %copy-done, bf16[16,32,128]{2,1,0:T(8,128)(2,1)S(1)} %copy-done.1, f32[3,2,4,16]{3,2,1,0:T(4,128)S(1)} %copy-done.6, s32[3,2,4,16]{3,2,1,0:T(4,128)S(1)} %copy-done.7, s32[3,2,4,16]{3,2,1,0:T(4,128)S(1)} %copy-done.8, ...), custom_call_target="tpu_custom_call" | custom-call | tf_op jit(solution)/shard_map/pallas_call | solution.py:415
  26.9 0.7 %copy.14 = f32[16,32,128]{2,1,0:T(8,128)} copy(f32[16,32,128]{2,1,0:T(8,128)S(1)} %get-tuple-element.4) | data formatting | bytes 524288
  27.6 0.6 %copy.15 = f32[3,2,4,16]{3,2,1,0:T(4,128)} copy(f32[3,2,4,16]{3,2,1,0:T(4,128)S(1)} %get-tuple-element.5) | data formatting | bytes 3072
Async XLA Ops:
  0.6 0.9 %copy-start = (bf16[16,32,128]{2,1,0:T(8,128)(2,1)S(1)}, bf16[16,32,128]{2,1,0:T(8,128)(2,1)}, u32[]{:S(2)}) copy-start(bf16[16,32,128]{2,1,0:T(8,128)(2,1)} %fixed.1) | copy-start | bytes 393220
  1.5 0.9 %copy-start.1 = (bf16[16,32,128]{2,1,0:T(8,128)(2,1)S(1)}, bf16[16,32,128]{2,1,0:T(8,128)(2,1)}, u32[]{:S(2)}) copy-start(bf16[16,32,128]{2,1,0:T(8,128)(2,1)} %moving.1) | copy-start | bytes 393220
  2.4 0.9 %copy-start.2 = (bf16[512,128]{1,0:T(8,128)(2,1)S(1)}, bf16[512,128]{1,0:T(8,128)(2,1)}, u32[]{:S(2)}) copy-start(bf16[512,128]{1,0:T(8,128)(2,1)} %constant.12.clone.table) | copy-start | bytes 393220
  3.3 0.9 %copy-start.3 = (bf16[384,128]{1,0:T(8,128)(2,1)S(1)}, bf16[384,128]{1,0:T(8,128)(2,1)}, u32[]{:S(2)}) copy-start(bf16[384,128]{1,0:T(8,128)(2,1)} %constant.14.clone.to_nodes) | copy-start | bytes 294916
  4.2 0.9 %copy-start.4 = (bf16[128,384]{1,0:T(8,128)(2,1)S(1)}, bf16[128,384]{1,0:T(8,128)(2,1)}, u32[]{:S(2)}) copy-start(bf16[128,384]{1,0:T(8,128)(2,1)} %constant.11.clone.from_nodes) | copy-start | bytes 294916
  5.1 0.8 %copy-start.5 = (bf16[128,128]{1,0:T(8,128)(2,1)S(1)}, bf16[128,128]{1,0:T(8,128)(2,1)}, u32[]{:S(2)}) copy-start(bf16[128,128]{1,0:T(8,128)(2,1)} %constant.10.clone.spread) | copy-start | bytes 98308
  5.9 0.7 %copy-start.6 = (f32[3,2,4,16]{3,2,1,0:T(4,128)S(1)}, f32[3,2,4,16]{3,2,1,0:T(4,128)}, u32[]{:S(2)}) copy-start(f32[3,2,4,16]{3,2,1,0:T(4,128)} %coarse.1) | copy-start | bytes 4612
  6.6 0.7 %copy-start.7 = (s32[3,2,4,16]{3,2,1,0:T(4,128)S(1)}, s32[3,2,4,16]{3,2,1,0:T(4,128)}, u32[]{:S(2)}) copy-start(s32[3,2,4,16]{3,2,1,0:T(4,128)} %codes.1) | copy-start | bytes 4612
  7.3 0.7 %copy-start.8 = (s32[3,2,4,16]{3,2,1,0:T(4,128)S(1)}, s32[3,2,4,16]{3,2,1,0:T(4,128)}, u32[]{:S(2)}) copy-start(s32[3,2,4,16]{3,2,1,0:T(4,128)} %offsets.1) | copy-start | bytes 4612
  8.0 0.7 %copy-start.9 = (bf16[32,128]{1,0:T(8,128)(2,1)S(1)}, bf16[32,128]{1,0:T(8,128)(2,1)}, u32[]{:S(2)}) copy-start(bf16[32,128]{1,0:T(8,128)(2,1)} %constant.13.clone.fold_y) | copy-start | bytes 24580

commit v2 on v1

--- a/solution.py
+++ b/solution.py
@@ -408,11 +408,28 @@
                 copies[d].wait_send()
 
 
+def write_out(residual, nodal, residual_out, nodal_out, sem):
+    copies = [
+        pltpu.make_async_copy(residual, residual_out, sem.at[0]),
+        pltpu.make_async_copy(nodal, nodal_out, sem.at[1]),
+    ]
+    for copy in copies:
+        copy.start()
+    for copy in copies:
+        copy.wait()
+
+
 def per_device(fixed_volume, moving_volume, coarse_motion, fraction_codes, block_offsets):
     hbm = pl.BlockSpec(memory_space=pltpu.HBM)
     vmem = pl.BlockSpec(memory_space=pltpu.VMEM)
     dma = pltpu.SemaphoreType.DMA
-    return pl.pallas_call(
+    hold = [
+        pltpu.with_memory_space_constraint(a, pltpu.HBM)
+        for a in (
+            fixed_volume, moving_volume, coarse_motion, fraction_codes, block_offsets, *constants()
+        )
+    ]
+    results = pl.pallas_call(
         body,
         out_shape=(
             jax.ShapeDtypeStruct((16, 32, 128), F32),
@@ -451,7 +468,17 @@
         compiler_params=pltpu.CompilerParams(
             collective_id=0, has_side_effects=True, vmem_limit_bytes=32 << 20
         ),
-    )(fixed_volume, moving_volume, coarse_motion, fraction_codes, block_offsets, *constants())
+    )(*hold)
+    return tuple(
+        pl.pallas_call(
+            write_out,
+            out_shape=[jax.ShapeDtypeStruct(r.shape, r.dtype) for r in results],
+            in_specs=[vmem, vmem],
+            out_specs=[hbm, hbm],
+            scratch_shapes=[dma((2,))],
+            compiler_params=pltpu.CompilerParams(vmem_limit_bytes=1 << 20),
+        )(*results)
+    )
 
 
 def solution(mesh):

time: 28.7 us -> 19.9 us (0.69); the launches traced: 28.2 us -> 19.8 us
  local copies, waits for them, and re-layouts: 9.37 us -> 0 us
  Pallas kernels: 18.1 us -> 19.1 us
    unnamed x22 -> x0, local copies, waits for them, and re-layouts: 9.37 us -> none
    pallas_call x0 -> x1, Pallas kernels: none -> 0.72 us  [per_device(): pl.pallas_call(write_out, out_shape=[jax.ShapeDtypeStruct(r.shape, r.dtyp...]
where the time goes in v2:
time: 19.9 us; the launch traced here: 19.8 us
  Pallas kernels  19.1 us (96%)
  between operations  0.64 us (3%)
    pallas_call x1, Pallas kernels, per_device(): pl.pallas_call(body, out_shape=(jax.ShapeDtypeStruct((16, 32, 128), F32),...  18.4 us
    pallas_call x1, Pallas kernels, per_device(): pl.pallas_call(write_out, out_shape=[jax.ShapeDtypeStruct(r.shape, r.dtyp...  0.72 us

profile of v2, /device:TPU:97, one launch (start us, length us, event | category | flops | bytes accessed | tf_op | source)
XLA Modules:
  0.0 19.8 jit_solution(17777830159054049358)
XLA Ops:
  0.6 18.4 %shard_map.113 = (f32[16,32,128]{2,1,0:T(8,128)S(1)}, f32[3,2,4,16]{3,2,1,0:T(4,128)S(1)}) custom-call(bf16[16,32,128]{2,1,0:T(8,128)(2,1)} %fixed.1, bf16[16,32,128]{2,1,0:T(8,128)(2,1)} %moving.1, f32[3,2,4,16]{3,2,1,0:T(4,128)} %coarse.1, s32[3,2,4,16]{3,2,1,0:T(4,128)} %codes.1, s32[3,2,4,16]{3,2,1,0:T(4,128)} %offsets.1, ...), custom_call_target="tpu_custom_call" | custom-call | tf_op jit(solution)/shard_map/pallas_call | solution.py:432
  19.1 0.7 %shard_map.114 = (f32[16,32,128]{2,1,0:T(8,128)}, f32[3,2,4,16]{3,2,1,0:T(4,128)}) custom-call(f32[16,32,128]{2,1,0:T(8,128)S(1)} %get-tuple-element.4.residual, f32[3,2,4,16]{3,2,1,0:T(4,128)S(1)} %get-tuple-element.5.nodal), custom_call_target="tpu_custom_call" | custom-call | tf_op jit(solution)/shard_map/pallas_call | solution.py:473
